TPU v7x, 32 devices: a whole 2x2x4 slice. The times are simulated.
32 devices in a mesh: fsdp: 8 (over z, x), seq: 4 (over y, core).
Axes of the slice: x: 2, y: 2, z: 4, core: 2. Of those that a mesh axis runs over, the one named last changes fastest.
Arguments:
- context: bfloat16 [16, 512, 2560], P('fsdp', 'seq'), may hold values from -6 to 6
- residual: bfloat16 [16, 512, 2560], P('fsdp', 'seq'), may hold values from -6 to 6
- target_rows: bfloat16 [16, 512, 2560], P('fsdp', 'seq'), may hold values from -0.00390625 to 0.00390625
- log_norm: float32 [16, 512], P('fsdp', 'seq'), may hold values from -0.15 to 0.15
- norm_gain: float32 [2560], replicated, may hold values from 0.1 to 1.9
- out_proj: bfloat16 [2560, 2560], P('fsdp'), may hold values from -0.125 to 0.125
- old_logprob: float32 [16, 512], P('fsdp', 'seq'), may hold values from -0.15 to 0.15
- lengths: int32 [16, 4], P('fsdp', 'seq'), may hold values from 112 to 128
- rewards: float32 [16, 4], P('fsdp', 'seq'), may hold values from -5 to 5
- prompt_ids: int32 [16, 4], P('fsdp', 'seq'), may hold values from 0 to 3, as said below
- placement: int32 [16, 4], P('fsdp', 'seq'), may hold values from 0 to 15, as said below
Outputs:
- grad_context: bfloat16 [16, 512, 2560], P('fsdp', 'seq')
- grad_weight: float32 [2560, 2560], P('fsdp')
- loss: float32 [], replicated
Inputs may be any that keep to these rules, and one draw needn't show every extreme that they name: `prompt_ids`: every prompt id names exactly 16 rows. Sampler row (a, s) goes to learner row (placement[a, s], s) and keeps a mod 2; the 2 rows of one device go to 2 different fsdp indices; every learner row receives exactly one row; in every column one of the 2 rows of each device goes 8 / 2 fsdp indices onward and another goes 1 index onward, counted round.
All inputs are finite; a program needn't handle non-finite values.
Results may differ from a plain program's by a relative error of at most 0.014.
Values may be sent and summed in bfloat16 or wider, within the bound.
A program may use at most 128 MiB of HBM per device.

v0:
```python
import math
import jax
import jax.numpy as jnp
from jax import lax
from jax.sharding import PartitionSpec as P

DW = 2560
AW = 2560
GS = 16


def body(
    context,
    residual,
    target_rows,
    log_norm,
    norm_gain,
    out_proj,
    old_logprob,
    lengths,
    rewards,
    prompt_ids,
    placement,
):
    nrows = context.shape[0]
    lmax = context.shape[1]
    fsdp_ways = lax.axis_size("fsdp")
    seq_ways = lax.axis_size("seq")
    prompts = nrows * fsdp_ways * seq_ways // GS
    all_tokens = nrows * lmax * fsdp_ways * seq_ways
    reward_flat = rewards.reshape(-1)
    prompt_flat = prompt_ids.reshape(-1)
    length_flat = lengths.reshape(-1)
    dest_flat = placement.reshape(-1)
    prompt_range = jnp.arange(prompts, dtype=jnp.int32)
    local_hot = (prompt_flat[:, None] == prompt_range[None, :]).astype(jnp.float32)
    group_sum, group_sq, count = lax.psum(
        (
            jnp.sum(local_hot * reward_flat[:, None], axis=0),
            jnp.sum(local_hot * (reward_flat * reward_flat)[:, None], axis=0),
            jnp.sum(length_flat.astype(jnp.float32)),
        ),
        ("fsdp", "seq"),
    )
    group_mean = group_sum / GS
    group_var = group_sq / GS - group_mean * group_mean
    row_mean = jnp.sum(local_hot * group_mean[None, :], axis=1)
    row_var = jnp.sum(local_hot * group_var[None, :], axis=1)
    advantage = (reward_flat - row_mean) / jnp.sqrt(row_var + 0.25)
    slots = jnp.arange(nrows, dtype=jnp.int32)
    every_old, every_adv, every_len, every_dest = (
        lax.all_gather(old_logprob, "fsdp", axis=0, tiled=True),
        lax.all_gather(advantage, "fsdp", axis=0, tiled=True),
        lax.all_gather(length_flat, "fsdp", axis=0, tiled=True),
        lax.all_gather(dest_flat, "fsdp", axis=0, tiled=True),
    )
    wanted = lax.axis_index("fsdp") * nrows + slots
    chosen = every_dest[None, :] == wanted[:, None]
    learn_old = jnp.sum(jnp.where(chosen[:, :, None], every_old[None, :, :], 0.0), axis=1)
    learn_adv = jnp.sum(jnp.where(chosen, every_adv[None, :], 0.0), axis=1)
    learn_len = jnp.sum(jnp.where(chosen, every_len[None, :], 0), axis=1)
    offsets = jnp.arange(lmax, dtype=jnp.int32)
    valid = (offsets[None, :] < learn_len[:, None]).astype(jnp.float32).reshape(-1)
    token_adv = jnp.broadcast_to(learn_adv[:, None], (nrows, lmax)).reshape(-1)
    tokens = nrows * lmax
    context_flat = context.reshape(tokens, AW)
    whole = lax.all_gather(out_proj, "fsdp", axis=0, tiled=True)
    hidden = residual.reshape(tokens, DW).astype(jnp.float32) + jnp.dot(
        context_flat, whole, preferred_element_type=jnp.float32
    )
    rinv = lax.rsqrt(jnp.mean(hidden * hidden, axis=1) + 1e-06)
    vecs = norm_gain[None, :] * target_rows.reshape(tokens, DW).astype(jnp.float32)
    hv_sum = jnp.sum(hidden * vecs, axis=1)
    score = hv_sum * rinv
    ratio = jnp.exp(score - log_norm.reshape(-1) - learn_old.reshape(-1))
    plain = ratio * token_adv
    clipped = jnp.clip(ratio, 0.8, 1.2) * token_adv
    objective = jnp.minimum(plain, clipped)
    loss_local = jnp.sum(valid * -objective)
    dscore = -valid * jnp.where(plain <= clipped, plain, 0.0) / count
    dhid = (dscore * rinv)[:, None] * (vecs - hidden * (rinv * rinv * hv_sum / DW)[:, None])
    grad_hidden = (dhid * (32.0 * all_tokens * math.sqrt(DW))).astype(jnp.bfloat16)
    grad_context = lax.dot_general(
        grad_hidden, whole, (((1,), (1,)), ((), ())), preferred_element_type=jnp.float32
    ).astype(jnp.bfloat16)
    piece = lax.psum_scatter(
        lax.dot_general(
            context_flat, grad_hidden, (((0,), (0,)), ((), ())), preferred_element_type=jnp.float32
        ).astype(jnp.bfloat16),
        "fsdp",
        scatter_dimension=0,
        tiled=True,
    )
    grad_weight = lax.psum(piece, "seq").astype(jnp.float32) * (1.0 / math.sqrt(all_tokens))
    loss = lax.psum(loss_local, ("fsdp", "seq")) / count
    return (grad_context.reshape(nrows, lmax, AW), grad_weight, loss)


def solution(mesh):
    return jax.shard_map(
        body,
        mesh=mesh,
        in_specs=(
            P("fsdp", "seq", None),
            P("fsdp", "seq", None),
            P("fsdp", "seq", None),
            P("fsdp", "seq"),
            P(),
            P("fsdp", None),
            P("fsdp", "seq"),
            P("fsdp", "seq"),
            P("fsdp", "seq"),
            P("fsdp", "seq"),
            P("fsdp", "seq"),
        ),
        out_specs=(P("fsdp", "seq", None), P("fsdp", None), P()),
        check_vma=False,
    )
```

profile of v0, /device:TPU:0, one launch (start us, length us, event | category | flops | bytes accessed | tf_op | source)
XLA Modules:
  0.0 559.2 jit_solution(6872598172934750625)
XLA Ops:
  7.2 0.7 all-gather.5.cloned.1.call-update
  7.9 0.0 reduce-scatter.4.cloned.1.call-start
  8.0 0.7 multiply_bitcast_fusion
  8.6 0.8 select_reduce_fusion.6
  9.4 46.3 %all-reduce.5 = (f32[4]{0:T(128)S(1)}, f32[4]{0:T(128)S(1)}) all-reduce(f32[4]{0:T(128)S(1)} %get-tuple-element.16, f32[4]{0:T(128)S(1)} %get-tuple-element.17), channel_id=1, replica_groups=mesh['fsdp'=8,'seq'=4] {'fsdp','seq'}, use_global_device_ids=true, to_apply=%region_5.0 | all-reduce | flops 8 | bytes 64 | tf_op jit(solution)/shard_map/psum | solution.py:37
  55.7 1.2 dynamic-slice
  57.6 0.9 select_reduce_fusion.5
  58.5 0.8 bitcast_dynamic-update-slice_fusion.1
  59.2 0.7 multiply_dynamic-update-slice_fusion
  60.0 0.7 bitcast_dynamic-update-slice_fusion
  60.7 20.1 %all-reduce.2 = f32[16]{0:T(128)S(1)} all-reduce(f32[16]{0:T(128)S(1)} %multiply_dynamic-update-slice_fusion), channel_id=1, replica_groups=mesh['fsdp'=8,'seq'=4] {'fsdp'}, use_global_device_ids=true, to_apply=%add.2 | all-reduce | flops 16 | bytes 128
  80.9 12.8 %all-reduce.3 = (s32[16]{0:T(128)S(1)}, s32[16]{0:T(128)S(1)}) all-reduce(s32[16]{0:T(128)S(1)} %bitcast_dynamic-update-slice_fusion.1, s32[16]{0:T(128)S(1)} %bitcast_dynamic-update-slice_fusion), channel_id=2, replica_groups=mesh['fsdp'=8,'seq'=4] {'fsdp'}, use_global_device_ids=true, to_apply=%add | all-reduce | flops 32 | bytes 256
  93.7 18.2 %all-gather.2 = f32[8,2,128]{2,1,0:T(2,128)S(1)} all-gather(f32[1,2,128]{2,1,0:T(2,128)} %bitcast.68), channel_id=1, replica_groups=mesh['fsdp'=8,'seq'=4] {'fsdp'}, dimensions={0}, use_global_device_ids=true | all-gather | bytes 9216 | tf_op jit(solution)/shard_map/all_gather | solution.py:52
  111.9 1.3 convert_reduce_fusion
  113.1 0.2 select_reduce_fusion.2
  113.3 0.1 select_reduce_fusion.7
  113.4 0.1 select_reduce_fusion
  113.5 83.5 %all-gather.5.cloned.1.call-done = bf16[2560,2560]{1,0:T(8,128)(2,1)} async-done(((bf16[320,2560]{1,0:T(8,128)(2,1)}), bf16[2560,2560]{1,0:T(8,128)(2,1)}) %all-gather.5.cloned.1.call-update) | async-done | bytes 13107216 | tf_op jit(solution)/shard_map/all_gather | solution.py:67
  197.0 10.4 %multiply_reduce_fusion = (f32[256]{0:T(256)S(1)}, f32[256]{0:T(256)S(1)}, f32[256,2560]{1,0:T(8,128)}) fusion(bf16[2,128,2560]{2,1,0:T(8,128)(2,1)} %param.13, f32[2560]{0:T(1024)} %param.15, bf16[256,2560]{1,0:T(8,128)(2,1)S(1)} %bitcast.62, bf16[2560,2560]{1,0:T(8,128)(2,1)} %all-gather.5.cloned.1.call-done, bf16[256,2560]{1,0:T(8,128)(2,1)} %bitcast.69), kind=kOutput, calls=%fused_computation.12 | convolution fusion | flops 3360685568 | bytes 19673088 | tf_op jit(solution)/shard_map/dot_general | solution.py:68
  207.4 0.7 select_reduce_fusion.1
  208.1 38.7 %all-reduce.4 = (f32[]{:T(128)}, f32[]{:T(128)}) all-reduce(f32[]{:T(128)} %convert_reduce_fusion, f32[]{:T(128)} %select_reduce_fusion.1), channel_id=1, replica_groups=mesh['fsdp'=8,'seq'=4] {'fsdp','seq'}, use_global_device_ids=true, to_apply=%region_12.13 | all-reduce | flops 2 | bytes 16 | tf_op jit(solution)/shard_map/psum | solution.py:37
  246.7 0.7 divide_multiply_fusion
  247.5 2.7 fusion.6
  250.2 6.8 %fusion = bf16[2560,2560]{0,1:T(8,128)(2,1)} fusion(bf16[256,2560]{1,0:T(8,128)(2,1)S(1)} %fusion.6, bf16[256,2560]{1,0:T(8,128)(2,1)S(1)} %bitcast.63), kind=kOutput, calls=%fused_computation.1 | convolution fusion | flops 3361996800 | bytes 15728640 | tf_op jit(solution)/shard_map/dot_general | solution.py:87
  257.0 17.6 %copy.17 = bf16[2560,2560]{1,0:T(8,128)(2,1)} copy(bf16[2560,2560]{0,1:T(8,128)(2,1)} %fusion) | data formatting | bytes 26214400
  274.6 0.0 all-reduce.8.cloned.1.call-start
  276.0 214.2 %reduce-scatter.4.cloned.1.call-done = bf16[320,2560]{1,0:T(8,128)(2,1)} async-done(((bf16[2560,2560]{1,0:T(8,128)(2,1)}), bf16[320,2560]{1,0:T(8,128)(2,1)}) %reduce-scatter.4.cloned.1.call-update) | async-done | bytes 1638416
  490.2 3.8 copy.18
  494.0 9.4 %convolution_convert_fusion.1 = bf16[256,2560]{1,0:T(8,128)(2,1)} fusion(bf16[256,2560]{1,0:T(8,128)(2,1)S(1)} %fusion.6, bf16[2560,2560]{1,0:T(8,128)(2,1)} %all-gather.5.cloned.1.call-done), kind=kOutput, calls=%fused_computation.4 | convolution fusion | flops 3356098560 | bytes 15728640 | tf_op jit(solution)/shard_map/dot_general | solution.py:83
  503.4 39.1 %all-reduce.8.cloned.1.call-done = bf16[320,2560]{0,1:T(8,128)(2,1)} async-done(((bf16[320,2560]{0,1:T(8,128)(2,1)}), bf16[320,2560]{0,1:T(8,128)(2,1)}) %all-reduce.8.cloned.1.call-update) | async-done | bytes 1638416 | tf_op jit(solution)/shard_map/psum | solution.py:94
  542.6 3.8 convert_multiply_fusion
  546.3 5.2 copy.16
  (14 shorter events, 0.1 us)
Async XLA Ops:
  7.2 189.9 %copy-start = (bf16[2,128,2560]{2,1,0:T(8,128)(2,1)S(1)}, bf16[2,128,2560]{2,1,0:T(8,128)(2,1)}, u32[]{:S(2)}) copy-start(bf16[2,128,2560]{2,1,0:T(8,128)(2,1)} %param.11) | copy-start | bytes 3932164
  7.2 189.9 %all-gather.5.cloned.1.call-start = ((), (), s32[]{:S(2)}) async-start(), calls=%async_computation.1 | async-start | bytes 14745600 | tf_op jit(solution)/shard_map/all_gather | solution.py:67
  7.9 482.3 %reduce-scatter.4.cloned.1.call-start = ((), (), s32[]{:S(2)}) async-start(), calls=%async_computation.3 | async-start | bytes 14745600
  197.0 10.4 %copy-start.2 = (f32[2,128]{1,0:T(2,128)S(1)}, f32[2,128]{1,0:T(2,128)}, u32[]{:S(2)}) copy-start(f32[2,128]{1,0:T(2,128)} %param.14) | copy-start | bytes 3076
  197.0 50.4 %copy-start.1 = (f32[2560]{0:T(1024)S(1)}, f32[2560]{0:T(1024)}, u32[]{:S(2)}) copy-start(f32[2560]{0:T(1024)} %param.15) | copy-start | bytes 30724
  274.6 267.9 %all-reduce.8.cloned.1.call-start = ((), (), s32[]{:S(2)}) async-start(), calls=%async_computation.2 | async-start | bytes 3932160 | tf_op jit(solution)/shard_map/psum | solution.py:94
Sparse Core Ops, SparseCore 0:
  10.2 186.7 all-gather.4
  274.7 215.4 reduce-scatter.3
  494.2 48.3 all-reduce.7
where the time goes:
time: 560 us; the launch traced here: 559 us
  waiting for transfers between devices  338 us (60%)
  blocking collectives  136 us (24%)
  local copies, waits for them, and re-layouts  29.4 us (5%)
  matrix products  26.5 us (5%)
  between operations  16.9 us (3%)
  other arithmetic  12.6 us (2%)
    unnamed x4, waiting for transfers between devices  215 us
    psum x2, blocking collectives, body(): lax.psum((jnp.sum(local_hot * reward_flat[:, None], axis=0), jnp.sum(loca...  85 us
    all_gather x1, waiting for transfers between devices, body(): whole = lax.all_gather(out_proj, 'fsdp', axis=0, tiled=True)  83.5 us
    psum x1, waiting for transfers between devices, body(): lax.psum(piece, 'seq').astype(jnp.float32) * (1.0 / math.sqrt(all_tokens))  39.1 us
    unnamed x2, blocking collectives  33 us
    unnamed x15, local copies, waits for them, and re-layouts  29.4 us
    all_gather x1, blocking collectives, body(): lax.all_gather(old_logprob, 'fsdp', axis=0, tiled=True)  18.2 us
  transfers between devices with their start and end apart: 3, of which 3 were waited for; matrix products, arithmetic and copies ran while one was open for 3% of the time, Pallas kernels for 0%

commit v1 on v0

--- a/solution.py
+++ b/solution.py
@@ -1,3 +1,4 @@
+import functools
 import math
 import jax
 import jax.numpy as jnp
@@ -7,6 +8,15 @@
 DW = 2560
 AW = 2560
 GS = 16
+
+
+def return_all_keys_in(view, ax_name, dev_axis):
+    for b in (ax_name, dev_axis):
+        view = lax.psum(view, axis_name=b)
+    return view
+
+
+scan_axis_part = functools.partial(return_all_keys_in, ax_name="seq", dev_axis="fsdp")
 
 
 def body(
@@ -34,13 +44,12 @@
     dest_flat = placement.reshape(-1)
     prompt_range = jnp.arange(prompts, dtype=jnp.int32)
     local_hot = (prompt_flat[:, None] == prompt_range[None, :]).astype(jnp.float32)
-    group_sum, group_sq, count = lax.psum(
+    group_sum, group_sq, count = scan_axis_part(
         (
             jnp.sum(local_hot * reward_flat[:, None], axis=0),
             jnp.sum(local_hot * (reward_flat * reward_flat)[:, None], axis=0),
             jnp.sum(length_flat.astype(jnp.float32)),
-        ),
-        ("fsdp", "seq"),
+        )
     )
     group_mean = group_sum / GS
     group_var = group_sq / GS - group_mean * group_mean

time: 560 us -> 515 us (0.920)
  waiting for transfers between devices: 338 us -> 308 us
  blocking collectives: 136 us -> 123 us
    unnamed x4, waiting for transfers between devices: 215 us -> 170 us
    unnamed x2 -> x1, blocking collectives: 33 us -> 8.75 us
    all_gather x1, waiting for transfers between devices: 83.5 us -> 99 us  [body(): whole = lax.all_gather(out_proj, 'fsdp', axis=0, tiled=True)]
    psum x2 -> x4, blocking collectives: 85 us -> 91.9 us  [the longest x3 49.8 us: return_all_keys_in(): view = lax.psum(view, axis_name=b)]
    unnamed x15 -> x17, local copies, waits for them, and re-layouts: 29.4 us -> 29.4 us
where the time goes in v1:
time: 515 us; the launch traced here: 514 us
  waiting for transfers between devices  308 us (60%)
  blocking collectives  123 us (24%)
  local copies, waits for them, and re-layouts  29.4 us (6%)
  matrix products  25.5 us (5%)
  between operations  16.9 us (3%)
  other arithmetic  10.5 us (2%)
    unnamed x4, waiting for transfers between devices  170 us
    all_gather x1, waiting for transfers between devices, body(): whole = lax.all_gather(out_proj, 'fsdp', axis=0, tiled=True)  99 us
    psum x3, blocking collectives, return_all_keys_in(): view = lax.psum(view, axis_name=b)  49.8 us
    psum x1, blocking collectives, body(): loss = lax.psum(loss_local, ('fsdp', 'seq')) / count  42.1 us
    psum x1, waiting for transfers between devices, body(): lax.psum(piece, 'seq').astype(jnp.float32) * (1.0 / math.sqrt(all_tokens))  39.1 us
    unnamed x17, local copies, waits for them, and re-layouts  29.4 us
    all_gather x1, blocking collectives, body(): lax.all_gather(old_logprob, 'fsdp', axis=0, tiled=True)  22.8 us
  transfers between devices with their start and end apart: 3, of which 3 were waited for; matrix products, arithmetic and copies ran while one was open for 3% of the time, Pallas kernels for 0%

profile of v1, /device:TPU:0, one launch (start us, length us, event | category | flops | bytes accessed | tf_op | source)
XLA Modules:
  0.0 514.3 jit_solution(12142992902419565538)
XLA Ops:
  7.2 0.7 all-gather.5.cloned.1.call-update
  8.0 1.3 convert_reduce_fusion
  9.2 0.7 multiply_bitcast_fusion
  9.9 0.8 select_reduce_fusion.6
  10.6 9.0 %all-reduce.6 = (f32[]{:T(128)}, f32[4]{0:T(128)S(1)}, f32[4]{0:T(128)S(1)}) all-reduce(f32[]{:T(128)} %convert_reduce_fusion, f32[4]{0:T(128)S(1)} %get-tuple-element.16, f32[4]{0:T(128)S(1)} %get-tuple-element.17), channel_id=1, replica_groups=mesh['fsdp'=8,'seq'=4] {'seq'}, use_global_device_ids=true, to_apply=%region_14.15 | all-reduce | flops 9 | bytes 72 | tf_op jit(solution)/shard_map/psum | solution.py:15
  19.6 22.4 %all-reduce.5 = (f32[4]{0:T(128)S(1)}, f32[4]{0:T(128)S(1)}) all-reduce(f32[4]{0:T(128)S(1)} %get-tuple-element.25, f32[4]{0:T(128)S(1)} %get-tuple-element.26), channel_id=1, replica_groups=mesh['fsdp'=8,'seq'=4] {'fsdp'}, use_global_device_ids=true, to_apply=%region_6.0 | all-reduce | flops 8 | bytes 64 | tf_op jit(solution)/shard_map/psum | solution.py:15
  42.1 1.2 dynamic-slice
  44.0 0.9 select_reduce_fusion.5
  44.8 0.8 bitcast_dynamic-update-slice_fusion
  45.6 0.7 bitcast_dynamic-update-slice_fusion.1
  46.3 0.7 multiply_dynamic-update-slice_fusion
  47.1 18.4 %all-reduce.4 = (f32[]{:T(128)}, f32[16]{0:T(128)S(1)}) all-reduce(f32[]{:T(128)} %get-tuple-element.24, f32[16]{0:T(128)S(1)} %multiply_dynamic-update-slice_fusion), channel_id=1, replica_groups=mesh['fsdp'=8,'seq'=4] {'fsdp'}, use_global_device_ids=true, to_apply=%region_15.16 | all-reduce | flops 17 | bytes 136 | tf_op jit(solution)/shard_map/psum | solution.py:15
  65.5 8.8 %all-reduce.3 = (s32[16]{0:T(128)S(1)}, s32[16]{0:T(128)S(1)}) all-reduce(s32[16]{0:T(128)S(1)} %bitcast_dynamic-update-slice_fusion.1, s32[16]{0:T(128)S(1)} %bitcast_dynamic-update-slice_fusion), channel_id=2, replica_groups=mesh['fsdp'=8,'seq'=4] {'fsdp'}, use_global_device_ids=true, to_apply=%add | all-reduce | flops 32 | bytes 256
  74.2 22.8 %all-gather.2 = f32[8,2,128]{2,1,0:T(2,128)S(1)} all-gather(f32[1,2,128]{2,1,0:T(2,128)} %bitcast.68), channel_id=1, replica_groups=mesh['fsdp'=8,'seq'=4] {'fsdp'}, dimensions={0}, use_global_device_ids=true | all-gather | bytes 9216 | tf_op jit(solution)/shard_map/all_gather | solution.py:61
  97.0 0.2 select_reduce_fusion.2
  97.2 0.1 select_reduce_fusion.7
  97.3 0.1 select_reduce_fusion
  97.4 99.0 %all-gather.5.cloned.1.call-done = bf16[2560,2560]{1,0:T(8,128)(2,1)} async-done(((bf16[320,2560]{1,0:T(8,128)(2,1)}), bf16[2560,2560]{1,0:T(8,128)(2,1)}) %all-gather.5.cloned.1.call-update) | async-done | bytes 13107216 | tf_op jit(solution)/shard_map/all_gather | solution.py:76
  196.4 9.3 %multiply_reduce_fusion = (f32[256]{0:T(256)S(1)}, f32[256]{0:T(256)S(1)}, f32[256,2560]{1,0:T(8,128)S(1)}) fusion(bf16[2,128,2560]{2,1,0:T(8,128)(2,1)} %param.13, f32[2560]{0:T(1024)} %param.15, bf16[256,2560]{1,0:T(8,128)(2,1)S(1)} %bitcast.62, bf16[2560,2560]{1,0:T(8,128)(2,1)} %all-gather.5.cloned.1.call-done, bf16[256,2560]{1,0:T(8,128)(2,1)} %bitcast.69), kind=kOutput, calls=%fused_computation.12 | convolution fusion | flops 3360685568 | bytes 19673088 | tf_op jit(solution)/shard_map/dot_general | solution.py:77
  205.8 0.7 divide_multiply_fusion
  206.5 0.7 fusion.6
  207.2 6.8 %fusion = bf16[2560,2560]{0,1:T(8,128)(2,1)} fusion(bf16[256,2560]{1,0:T(8,128)(2,1)S(1)} %fusion.6, bf16[256,2560]{1,0:T(8,128)(2,1)S(1)} %bitcast.63), kind=kOutput, calls=%fused_computation.1 | convolution fusion | flops 3361996800 | bytes 15728640 | tf_op jit(solution)/shard_map/dot_general | solution.py:96
  214.0 17.6 %copy.17 = bf16[2560,2560]{1,0:T(8,128)(2,1)} copy(bf16[2560,2560]{0,1:T(8,128)(2,1)} %fusion) | data formatting | bytes 26214400
  231.7 0.0 all-reduce.9.cloned.1.call-start
  231.7 0.7 select_reduce_fusion.1
  232.4 42.1 %psum.63 = f32[]{:T(128)} all-reduce(f32[]{:T(128)} %select_reduce_fusion.1), channel_id=1, replica_groups=mesh['fsdp'=8,'seq'=4] {'fsdp','seq'}, use_global_device_ids=true, to_apply=%region_19.20 | all-reduce | flops 1 | bytes 8 | tf_op jit(solution)/shard_map/psum | solution.py:104
  275.8 169.4 %reduce-scatter.4.cloned.1.call-done = bf16[320,2560]{1,0:T(8,128)(2,1)} async-done(((bf16[2560,2560]{1,0:T(8,128)(2,1)}), bf16[320,2560]{1,0:T(8,128)(2,1)}) %reduce-scatter.4.cloned.1.call-update) | async-done | bytes 1638416
  445.3 3.8 copy.18
  449.1 9.4 %convolution_convert_fusion.1 = bf16[256,2560]{1,0:T(8,128)(2,1)} fusion(bf16[256,2560]{1,0:T(8,128)(2,1)S(1)} %fusion.6, bf16[2560,2560]{1,0:T(8,128)(2,1)} %all-gather.5.cloned.1.call-done), kind=kOutput, calls=%fused_computation.4 | convolution fusion | flops 3356098560 | bytes 15728640 | tf_op jit(solution)/shard_map/dot_general | solution.py:92
  458.5 39.1 %all-reduce.9.cloned.1.call-done = bf16[320,2560]{0,1:T(8,128)(2,1)} async-done(((bf16[320,2560]{0,1:T(8,128)(2,1)}), bf16[320,2560]{0,1:T(8,128)(2,1)}) %all-reduce.9.cloned.1.call-update) | async-done | bytes 1638416 | tf_op jit(solution)/shard_map/psum | solution.py:103
  497.6 3.8 convert_multiply_fusion
  501.4 5.2 %copy.16 = f32[320,2560]{1,0:T(8,128)} copy(f32[320,2560]{0,1:T(8,128)} %convert_multiply_fusion) | data formatting | bytes 6553600
  (17 shorter events, 0.1 us)
Async XLA Ops:
  7.2 189.3 %copy-start = (bf16[2,128,2560]{2,1,0:T(8,128)(2,1)S(1)}, bf16[2,128,2560]{2,1,0:T(8,128)(2,1)}, u32[]{:S(2)}) copy-start(bf16[2,128,2560]{2,1,0:T(8,128)(2,1)} %param.11) | copy-start | bytes 3932164
  7.2 189.3 %all-gather.5.cloned.1.call-start = ((), (), s32[]{:S(2)}) async-start(), calls=%async_computation.1 | async-start | bytes 14745600 | tf_op jit(solution)/shard_map/all_gather | solution.py:76
  7.9 437.4 %reduce-scatter.4.cloned.1.call-start = ((), (), s32[]{:S(2)}) async-start(), calls=%async_computation.3 | async-start | bytes 14745600
  196.4 9.4 %copy-start.3 = (f32[2,128]{1,0:T(2,128)S(1)}, f32[2,128]{1,0:T(2,128)}, u32[]{:S(2)}) copy-start(f32[2,128]{1,0:T(2,128)} %param.14) | copy-start | bytes 3076
  196.4 10.1 %copy-start.1 = (bf16[2,128,2560]{2,1,0:T(8,128)(2,1)S(1)}, bf16[2,128,2560]{2,1,0:T(8,128)(2,1)}, u32[]{:S(2)}) copy-start(bf16[2,128,2560]{2,1,0:T(8,128)(2,1)} %param.13) | copy-start | bytes 3932164
  196.4 10.1 %copy-start.2 = (f32[2560]{0:T(1024)S(1)}, f32[2560]{0:T(1024)}, u32[]{:S(2)}) copy-start(f32[2560]{0:T(1024)} %param.15) | copy-start | bytes 30724
  231.7 266.0 %all-reduce.9.cloned.1.call-start = ((), (), s32[]{:S(2)}) async-start(), calls=%async_computation.2 | async-start | bytes 3932160 | tf_op jit(solution)/shard_map/psum | solution.py:103
Sparse Core Ops, SparseCore 0:
  10.2 186.1 all-gather.4
  231.8 213.4 reduce-scatter.3
  449.3 48.3 all-reduce.8
